TPU v7x, 256 devices: a whole 4x4x8 slice. The times are simulated.
256 devices in a mesh: depth: 8 (over x_lo, y), row: 32 (over x_hi, z, core).
Axes of the slice: x: 4 (x_hi: 2, x_lo: 2; x = x_hi * 2 + x_lo), y: 4, z: 8, core: 2. Of those that a mesh axis runs over, the one named last changes fastest.
Arguments:
- field: float32 [2, 8, 4096, 4096], P(None, 'depth', 'row'), may hold values from -6 to 6
- hologram: float32 [4096, 4096], P('row'), may hold values from -16 to 16
- defocus: float32 [8], P('depth'), may hold values from 512 to 2048
Outputs:
- estimate: float32 [2, 8, 4096, 4096], P(None, 'depth', 'row')
All inputs are finite; a program needn't handle non-finite values.
Results may differ from a plain program's by a relative error of at most 0.00045.
Values sent between devices are 32-bit elements; how exact they have to be, the bound alone decides.
A program may use at most 320 MiB of HBM per device.

v0:
```python
import math
import jax
import jax.numpy as jnp
from jax import lax
from jax.sharding import PartitionSpec as P

tv_step_size = 1.0 / 12.0
tv_sharpness = 0.25


def passed_along(block, axis, distance):
    devices = range(lax.axis_size(axis))
    route = [(i - distance, i) for i in devices if i - distance in devices]
    return lax.ppermute(block, axis, route)


def split_length(length_total):
    smaller = 1
    candidate = 1
    while candidate * candidate <= length_total:
        if length_total % candidate == 0:
            smaller = candidate
        candidate = candidate + 1
    return (smaller, length_total // smaller)


def block_table(cosines, sines):
    return jnp.stack([jnp.stack([cosines, -sines]), jnp.stack([sines, cosines])])


def dft_tables(length_total, inverse):
    outer_len, inner_len = split_length(length_total)
    direction = 2.0 * math.pi if inverse else -2.0 * math.pi
    first_k = jnp.arange(outer_len, dtype=jnp.int32)[:, None]
    first_a = jnp.arange(outer_len, dtype=jnp.int32)[None, :]
    radians_one = (first_k * first_a % outer_len).astype(jnp.float32) * (direction / outer_len)
    first_table = block_table(jnp.cos(radians_one), jnp.sin(radians_one))
    second_k = jnp.arange(outer_len, dtype=jnp.int32)[:, None, None]
    second_b = jnp.arange(inner_len, dtype=jnp.int32)[None, :, None]
    second_m = jnp.arange(inner_len, dtype=jnp.int32)[None, None, :]
    whole_index = (second_k * second_b + second_b * second_m * outer_len) % length_total
    radians_two = whole_index.astype(jnp.float32) * (direction / length_total)
    scale = 1.0 / length_total if inverse else 1.0
    second_table = block_table(jnp.cos(radians_two) * scale, jnp.sin(radians_two) * scale)
    return (first_table, second_table, outer_len, inner_len)


def contract(formula, table, data):
    return jnp.einsum(
        formula, table, data, precision=lax.Precision.HIGHEST, preferred_element_type=jnp.float32
    )


def transform_last(data, tables, real_input, real_only):
    first_table, second_table, outer_len, inner_len = tables
    if real_input:
        data = data[None]
        first_table = first_table[:, :1]
    if real_only:
        second_table = second_table[:1]
    leading = data.shape[1:-1]
    folded = data.reshape((data.shape[0],) + leading + (outer_len, inner_len))
    middle = contract("rqka,q...ab->r...kb", first_table, folded)
    result = contract("rqkbm,q...kb->r...mk", second_table, middle)
    result = result.reshape((result.shape[0],) + leading + (outer_len * inner_len,))
    if real_only:
        return result[0]
    return result


def transform_rows(data, tables):
    first_table, second_table, outer_len, inner_len = tables
    leading = data.shape[1:-2]
    trailing = data.shape[-1]
    folded = data.reshape((2,) + leading + (outer_len, inner_len, trailing))
    middle = contract("rqka,q...abc->r...kbc", first_table, folded)
    result = contract("rqkbm,q...kbc->r...mkc", second_table, middle)
    return result.reshape((2,) + leading + (outer_len * inner_len, trailing))


def centred_squares(length_total, offset_start, length_part):
    indices = offset_start + jnp.arange(length_part, dtype=jnp.int32)
    centred = jnp.where(indices < length_total // 2, indices, indices - length_total)
    return (centred * centred).astype(jnp.float32)


def transfer_phase(depth_values, length_total, column_start, column_len):
    ky_squares = centred_squares(length_total, 0, length_total)
    kx_squares = centred_squares(length_total, column_start, column_len)
    grid_sum = (ky_squares[:, None] + kx_squares[None, :]) * (
        math.pi / (length_total * length_total)
    )
    return depth_values[:, None, None] * grid_sum[None]


def ahead_diff(values, incoming, axis_pos):
    extent = values.shape[axis_pos]
    shifted = jnp.concatenate(
        [lax.slice_in_dim(values, 1, extent, axis=axis_pos), incoming], axis=axis_pos
    )
    return shifted - values


def behind_diff(values, incoming, axis_pos):
    extent = values.shape[axis_pos]
    shifted = jnp.concatenate(
        [incoming, lax.slice_in_dim(values, 0, extent - 1, axis=axis_pos)], axis=axis_pos
    )
    return values - shifted


def flux_terms(depth_diff, row_diff, col_diff):
    magnitude = jnp.sqrt(
        jnp.sum(depth_diff * depth_diff + row_diff * row_diff + col_diff * col_diff, axis=0)
    )
    factor = 1.0 / (1.0 + tv_sharpness * magnitude)
    return (depth_diff * factor, row_diff * factor, col_diff * factor)


def shrink_shifts(moved_field, depth_index, row_index, plane_total, length_total):
    planes_dev = moved_field.shape[1]
    rows_dev = moved_field.shape[2]
    plane_next = passed_along(moved_field, "depth", -1)
    row_next = passed_along(moved_field[:, :, :1], "row", -1)
    plane_ids = depth_index * planes_dev + jnp.arange(planes_dev, dtype=jnp.int32)
    row_ids = row_index * rows_dev + jnp.arange(rows_dev, dtype=jnp.int32)
    depth_diff = jnp.where(
        (plane_ids == plane_total - 1)[None, :, None, None],
        0.0,
        ahead_diff(moved_field, plane_next, 1),
    )
    row_diff = jnp.where(
        (row_ids == length_total - 1)[None, None, :, None],
        0.0,
        ahead_diff(moved_field, row_next, 2),
    )
    col_diff = ahead_diff(moved_field, moved_field[..., -1:], 3)
    flux_z, flux_y, flux_x = flux_terms(depth_diff, row_diff, col_diff)
    prior_plane = passed_along(flux_z, "depth", 1)
    prior_row = passed_along(flux_y[:, :, -1:], "row", 1)
    divergence = (
        behind_diff(flux_z, prior_plane, 1)
        + behind_diff(flux_y, prior_row, 2)
        + behind_diff(flux_x, jnp.zeros_like(flux_x[..., :1]), 3)
    )
    return moved_field + tv_step_size * divergence


def per_device(field, hologram, defocus):
    planes_dev = field.shape[1]
    rows_dev = field.shape[2]
    length_total = field.shape[3]
    row_devices = lax.axis_size("row")
    depth_devices = lax.axis_size("depth")
    row_index = lax.axis_index("row")
    depth_index = lax.axis_index("depth")
    cols_dev = length_total // row_devices
    rows_piece = rows_dev // depth_devices
    plane_total = planes_dev * depth_devices
    forward_tables = dft_tables(length_total, False)
    inverse_tables = dft_tables(length_total, True)
    phase_table = transfer_phase(defocus, length_total, row_index * cols_dev, cols_dev)
    cosine_table = jnp.cos(phase_table)
    sine_table = jnp.sin(phase_table)
    hologram_part = lax.dynamic_slice_in_dim(hologram, depth_index * rows_piece, rows_piece, 0)
    estimate = field
    spectrum = transform_last(estimate, forward_tables, False, False)
    spectrum = lax.all_to_all(spectrum, "row", split_axis=3, concat_axis=2, tiled=True)
    spectrum = transform_rows(spectrum, forward_tables)
    sum_real = jnp.sum(spectrum[0] * cosine_table + spectrum[1] * sine_table, axis=0)
    sum_imag = jnp.sum(spectrum[1] * cosine_table - spectrum[0] * sine_table, axis=0)
    summed = transform_rows(jnp.stack([sum_real, sum_imag]), inverse_tables)
    by_rows = lax.all_to_all(summed, "row", split_axis=1, concat_axis=2, tiled=True)
    image_part = transform_last(by_rows, inverse_tables, False, True)
    image_sum = lax.psum_scatter(image_part, "depth", scatter_dimension=0, tiled=True)
    misfit = image_sum - hologram_part
    misfit_block = lax.all_gather(misfit, "depth", axis=0, tiled=True)
    misfit_pair = transform_last(misfit_block, forward_tables, True, False)
    misfit_spec = lax.all_to_all(misfit_pair, "row", split_axis=2, concat_axis=1, tiled=True)
    misfit_spec = transform_rows(misfit_spec, forward_tables)
    adj_real = misfit_spec[0][None] * cosine_table - misfit_spec[1][None] * sine_table
    adj_imag = misfit_spec[0][None] * sine_table + misfit_spec[1][None] * cosine_table
    adjoint = transform_rows(jnp.stack([adj_real, adj_imag]), inverse_tables)
    adjoint = lax.all_to_all(adjoint, "row", split_axis=2, concat_axis=3, tiled=True)
    gradient = transform_last(adjoint, inverse_tables, False, False)
    moved_field = estimate - 1.0 / plane_total * gradient
    estimate = shrink_shifts(moved_field, depth_index, row_index, plane_total, length_total)
    return estimate


def solution(mesh):
    return jax.shard_map(
        per_device,
        mesh=mesh,
        in_specs=(P(None, "depth", "row", None), P("row", None), P("depth")),
        out_specs=P(None, "depth", "row", None),
        check_vma=False,
    )
```

profile of v0, /device:TPU:34, one launch (start us, length us, event | category | flops | bytes accessed | tf_op | source)
XLA Modules:
  0.0 1049.4 jit_solution(16027976916007795739)
XLA Ops:
  12.7 17.3 %fusion.100 = (f32[1,64,64,64]{2,3,0,1:T(8,128)S(1)}, f32[1,64,64,64]{2,3,0,1:T(8,128)}, f32[1,64,64,64]{2,3,0,1:T(8,128)}, f32[1,64,64,64]{2,3,0,1:T(8,128)}, f...) fusion(s32[64,64]{0,1:T(8,128)S(1)} %broadcast_multiply_fusion.3, s32[64,64]{1,0:T(8,128)S(1)} %copy.91), kind=kLoop, calls=%fused_computation.103 | loop fusion | flops 4980736 | bytes 6324224 | tf_op jit(solution)/shard_map/neg | solution.py:28
  38.1 11.0 %fusion.46 = f32[2,1,128,64,64]{2,3,0,4,1:T(8,128)S(1)} fusion(f32[1,2,64,64,64]{3,4,1,0,2:T(8,128)S(1)} %get-tuple-element.13, f32[1,2,64,64,64]{3,4,1,0,2:T(8,128)S(1)} %get-tuple-element.12, f32[2,128,64,64,1]{1,2,3,0,4:T(8,128)S(1)} %fusion.43), kind=kOutput, calls=%fused_computation.64 | convolution fusion | flops 1611661312 | bytes 12582912 | tf_op jit(solution)/shard_map/rqkbm,q...kb->r...mk/dot_general | solution.py:49
  51.6 16.2 %copy.95 = f32[2,1,128,4096]{2,0,1,3:T(2,128)} copy(f32[2,1,128,4096]{2,3,0,1:T(8,128)S(1)} %bitcast.244) | data formatting | bytes 8388608 | tf_op jit(solution)/shard_map/reshape | solution.py:65
  67.8 10.3 all-to-all-start
  79.2 8.7 fusion.42
  87.9 85.5 %all-to-all-done = f32[2,1,128,4096]{2,0,1,3:T(2,128)} async-done(((f32[2,1,128,4096]{2,0,1,3:T(2,128)}), f32[2,1,128,4096]{2,0,1,3:T(2,128)}, u32[]{:S(2)}, u32[]{:S(2)}) %all-to-all-start) | async-done | bytes 4194336 | tf_op jit(solution)/shard_map/all_to_all | solution.py:168
  183.5 8.8 fusion.49
  192.4 10.0 fusion.52
  202.4 8.3 multiply_add_fusion.1
  214.6 10.4 fusion.76
  227.4 15.6 %copy.105 = f32[2,4096,128]{2,0,1:T(2,128)S(1)} copy(f32[2,4096,128]{2,1,0:T(8,128)S(1)} %bitcast.247) | data formatting | bytes 8388608 | tf_op jit(solution)/shard_map/reshape | solution.py:78
  243.1 105.9 %all_to_all.60 = f32[2,4096,128]{2,0,1:T(2,128)S(1)} all-to-all(f32[2,4096,128]{2,0,1:T(2,128)S(1)} %copy.105), channel_id=1, replica_groups=mesh['depth'=8,'row'=32] {'row'}, dimensions={1} | all-to-all | bytes 8388608 | tf_op jit(solution)/shard_map/all_to_all | solution.py:173
  356.9 8.8 fusion.58
  365.7 6.5 fusion.97
  378.4 39.3 %reduce-scatter.4.cloned.1.call-done = f32[16,4096]{1,0:T(8,128)} async-done(((f32[128,4096]{1,0:T(8,128)}), f32[16,4096]{1,0:T(8,128)}) %reduce-scatter.4.cloned.1.call-update) | async-done | bytes 262160
  426.7 43.0 %all-gather.2.cloned.1.call-done = f32[128,4096]{1,0:T(8,128)} async-done(((f32[16,4096]{1,0:T(8,128)}), f32[128,4096]{1,0:T(8,128)}) %all-gather.2.cloned.1.call-update) | async-done | bytes 2097168 | tf_op jit(solution)/shard_map/all_gather | solution.py:177
  476.6 12.6 %fusion.61 = f32[2,128,64,64]{1,2,0,3:T(8,128)S(1)} fusion(f32[1,2,64,64,64]{3,4,1,0,2:T(8,128)} %copy-done.6, f32[1,2,64,64,64]{3,4,1,0,2:T(8,128)S(1)} %copy-done.4, f32[2,128,64,64,1]{1,2,0,3,4:T(8,128)S(1)} %convolution_bitcast_fusion), kind=kOutput, calls=%fused_computation.69 | convolution fusion | flops 1611661312 | bytes 12582912 | tf_op jit(solution)/shard_map/rqkbm,q...kb->r...mk/dot_general | solution.py:49
  491.7 15.6 %copy.117 = f32[2,128,4096]{1,0,2:T(2,128)S(1)} copy(f32[2,128,4096]{1,2,0:T(8,128)S(1)} %bitcast.250) | data formatting | bytes 8388608 | tf_op jit(solution)/shard_map/reshape | solution.py:65
  507.3 107.2 %all_to_all.61 = f32[2,128,4096]{1,0,2:T(2,128)S(1)} all-to-all(f32[2,128,4096]{1,0,2:T(2,128)S(1)} %copy.117), channel_id=1, replica_groups=mesh['depth'=8,'row'=32] {'row'}, dimensions={2} | all-to-all | bytes 8388608 | tf_op jit(solution)/shard_map/all_to_all | solution.py:179
  622.4 8.7 fusion.64
  631.1 10.0 fusion.67
  641.1 8.3 multiply_subtract_fusion
  653.5 10.4 fusion.81
  666.3 15.6 %copy.127 = f32[2,1,4096,128]{3,0,1,2:T(2,128)S(1)} copy(f32[2,1,4096,128]{3,2,0,1:T(8,128)S(1)} %bitcast.252) | data formatting | bytes 8388608 | tf_op jit(solution)/shard_map/reshape | solution.py:78
  682.0 101.2 %all_to_all.62 = f32[2,1,4096,128]{3,0,1,2:T(2,128)S(1)} all-to-all(f32[2,1,4096,128]{3,0,1,2:T(2,128)S(1)} %copy.127), channel_id=1, replica_groups=mesh['depth'=8,'row'=32] {'row'}, dimensions={2} | all-to-all | bytes 8388608 | tf_op jit(solution)/shard_map/all_to_all | solution.py:184
  791.1 8.8 fusion.73
  799.9 10.0 fusion.11
  836.9 71.8 %collective-permute-done = f32[2,1,128,4096]{2,3,0,1:T(8,128)} collective-permute-done((f32[2,1,128,4096]{2,3,0,1:T(8,128)}, f32[2,1,128,4096]{2,3,0,1:T(8,128)}, u32[]{:S(2)}, u32[]{:S(2)}) %collective-permute-start) | collective-permute-done | bytes 4194336 | tf_op jit(solution)/shard_map/ppermute | solution.py:14
  908.7 9.1 add_reduce_fusion
  920.1 7.2 broadcast_multiply_fusion.2
  943.2 79.4 %collective-permute-done.2 = f32[2,1,128,4096]{2,3,0,1:T(8,128)} collective-permute-done((f32[2,1,128,4096]{2,3,0,1:T(8,128)}, f32[2,1,128,4096]{2,3,0,1:T(8,128)}, u32[]{:S(2)}, u32[]{:S(2)}) %collective-permute-start.2) | collective-permute-done | bytes 4194336 | tf_op jit(solution)/shard_map/ppermute | solution.py:14
  1022.6 14.0 %fusion.10 = f32[2,1,128,4096]{2,3,0,1:T(8,128)} fusion(f32[2,1,128,4096]{2,3,0,1:T(8,128)} %bitcast_subtract_fusion, f32[2,1,128,4096]{2,3,0,1:T(8,128)} %copy-done.9, f32[2,1,127,4096]{2,3,0,1:T(8,128)} %bitcast.239, f32[2,1,1,4096]{2,3,0,1:T(8,128)} %copy.138, f32[2,1,128,4096]{2,3,0,1:T(8,128)} %get-tuple-element.7, f32[2,1,128,4095]{2,3,0,1:T(8,128)} %bitcast.240, ...), kind=kLoop, calls=%fused_computation.21 | loop fusion | flops 8388608 | bytes 33553408 | tf_op jit(solution)/shard_map/add | solution.py:146
  (106 shorter events, 138.9 us)
Async XLA Ops:
  6.5 371.2 %copy-start = (f32[128,4096]{1,0:T(8,128)S(1)}, f32[128,4096]{1,0:T(8,128)}, u32[]{:S(2)}) copy-start(f32[128,4096]{1,0:T(8,128)} %param.4) | copy-start | bytes 6291460
  30.0 2.2 copy-start.16
  31.7 6.4 copy-start.2
  31.7 6.4 copy-start.6
  67.8 105.6 %all-to-all-start = ((f32[2,1,128,4096]{2,0,1,3:T(2,128)}), f32[2,1,128,4096]{2,0,1,3:T(2,128)}, u32[]{:S(2)}, u32[]{:S(2)}) async-start(f32[2,1,128,4096]{2,0,1,3:T(2,128)} %copy.95), calls=%async_computation | async-start | bytes 8388608 | tf_op jit(solution)/shard_map/all_to_all | solution.py:168
  78.2 339.5 %reduce-scatter.4.cloned.1.call-start = ((), (), s32[]{:S(2)}) async-start(), calls=%async_computation.6 | async-start | bytes 2359296
  183.5 8.8 copy-start.3
  183.5 8.8 copy-start.7
  210.6 3.9 copy-start.10
  210.7 3.9 copy-start.13
  356.9 8.8 copy-start.21
  356.9 8.8 copy-start.22
  377.7 92.0 %all-gather.2.cloned.1.call-start = ((), (), s32[]{:S(2)}) async-start(), calls=%async_computation.5 | async-start | bytes 2359296 | tf_op jit(solution)/shard_map/all_gather | solution.py:177
  471.9 4.8 copy-start.4
  622.4 8.7 copy-start.5
  622.4 8.7 copy-start.8
  649.4 4.1 copy-start.11
  649.4 4.1 copy-start.14
  791.0 8.8 copy-start.12
  791.0 8.8 copy-start.15
  809.9 2.7 copy-start.17
  815.0 93.8 %collective-permute-start = (f32[2,1,128,4096]{2,3,0,1:T(8,128)}, f32[2,1,128,4096]{2,3,0,1:T(8,128)}, u32[]{:S(2)}, u32[]{:S(2)}) collective-permute-start(f32[2,1,128,4096]{2,3,0,1:T(8,128)} %bitcast_subtract_fusion), channel_id=1, source_target_pairs={{32,0},{64,32},{96,64},{128,96},{160,128},{192,160},{224,192},{33,... | collective-permute-start | bytes 12582920 | tf_op jit(solution)/shard_map/ppermute | solution.py:14
  821.8 12.5 %collective-permute-start.1 = (f32[2,1,1,4096]{3,0,2,1:T(2,128)S(1)}, f32[2,1,1,4096]{3,0,2,1:T(2,128)S(1)}, u32[]{:S(2)}, u32[]{:S(2)}) collective-permute-start(f32[2,1,1,4096]{3,0,2,1:T(2,128)S(1)} %copy.135), channel_id=1, source_target_pairs={{1,0},{2,1},{3,2},{4,3},{5,4},{6,5},{7,6},{8,7},{9,8},{10,9},{11,1... | collective-permute-start | bytes 98312 | tf_op jit(solution)/shard_map/ppermute | solution.py:14
  908.7 9.9 copy-start.19
  908.7 9.9 copy-start.20
  917.8 2.3 copy-start.18
  927.3 2.0 copy-start.9
  927.3 95.3 %collective-permute-start.2 = (f32[2,1,128,4096]{2,3,0,1:T(8,128)}, f32[2,1,128,4096]{2,3,0,1:T(8,128)}, u32[]{:S(2)}, u32[]{:S(2)}) collective-permute-start(f32[2,1,128,4096]{2,3,0,1:T(8,128)} %get-tuple-element.5), channel_id=1, source_target_pairs={{0,32},{32,64},{64,96},{96,128},{128,160},{160,192},{192,224},{1,3... | collective-permute-start | bytes 12582920 | tf_op jit(solution)/shard_map/ppermute | solution.py:14
  935.3 5.2 collective-permute-start.3
  1022.6 19.6 %copy-start.1 = (f32[128,4096]{1,0:T(8,128)S(1)}, f32[128,4096]{1,0:T(8,128)}, u32[]{:S(2)}) copy-start(f32[128,4096]{1,0:T(8,128)} %param.4) | copy-start | bytes 6291460
Sparse Core Ops, SparseCore 0:
  377.8 39.8 reduce-scatter.3
  426.8 42.8 all-gather.1
where the time goes:
time: 1060 us; the launch traced here: 1050 us
  waiting for transfers between devices  322 us (30%)
  blocking collectives  314 us (30%)
  local copies, waits for them, and re-layouts  162 us (15%)
  matrix products  134 us (13%)
  other arithmetic  81.5 us (8%)
  starting transfers between devices  20.1 us (2%)
  between operations  15 us (1%)
    ppermute x4, waiting for transfers between devices, passed_along(): return lax.ppermute(block, axis, route)  155 us
    dot_general x16, matrix products, contract(): jnp.einsum(formula, table, data, precision=lax.Precision.HIGHEST, preferr...  134 us
    all_to_all x1, blocking collectives, per_device(): lax.all_to_all(misfit_pair, 'row', split_axis=2, concat_axis=1, tiled=True)  107 us
    all_to_all x1, blocking collectives, per_device(): lax.all_to_all(summed, 'row', split_axis=1, concat_axis=2, tiled=True)  106 us
    all_to_all x1, blocking collectives, per_device(): lax.all_to_all(adjoint, 'row', split_axis=2, concat_axis=3, tiled=True)  101 us
    all_to_all x1, waiting for transfers between devices, per_device(): lax.all_to_all(spectrum, 'row', split_axis=3, concat_axis=2, tiled=True)  85.5 us
    all_gather x1, waiting for transfers between devices, per_device(): misfit_block = lax.all_gather(misfit, 'depth', axis=0, tiled=True)  43 us
    unnamed x3, waiting for transfers between devices  39.3 us
  transfers between devices with their start and end apart: 7, of which 6 were waited for; matrix products, arithmetic and copies ran while one was open for 3% of the time, Pallas kernels for 0%

commit v1 on v0

--- a/solution.py
+++ b/solution.py
@@ -174,7 +174,9 @@
     image_part = transform_last(by_rows, inverse_tables, False, True)
     image_sum = lax.psum_scatter(image_part, "depth", scatter_dimension=0, tiled=True)
     misfit = image_sum - hologram_part
-    misfit_block = lax.all_gather(misfit, "depth", axis=0, tiled=True)
+    misfit_block = jnp.concatenate(
+        lax.all_to_all(jnp.stack([misfit] * lax.axis_size("depth")), "depth", 0, 0), axis=0
+    )
     misfit_pair = transform_last(misfit_block, forward_tables, True, False)
     misfit_spec = lax.all_to_all(misfit_pair, "row", split_axis=2, concat_axis=1, tiled=True)
     misfit_spec = transform_rows(misfit_spec, forward_tables)

time: 1060 us -> 1060 us (level)
  waiting for transfers between devices: 322 us -> 279 us
  blocking collectives: 314 us -> 340 us
    all_gather x1 -> x0, waiting for transfers between devices: 43 us -> none  [per_device(): misfit_block = lax.all_gather(misfit, 'depth', axis=0, tiled=True)]
    all_to_all x0 -> x1, blocking collectives: none -> 24.9 us  [per_device(): lax.all_to_all(jnp.stack([misfit] * lax.axis_size('depth')), 'depth', 0, 0)]
    unnamed x3 -> x2, waiting for transfers between devices: 39.3 us -> 39.9 us
  transfers between devices with their start and end apart: 7 -> 6, of which waited for: 6 -> 5; matrix products, arithmetic and copies ran while one was open for 3% -> 3% of each run, Pallas kernels for 0% -> 0%
where the time goes in v1:
time: 1060 us; the launch traced here: 1050 us
  blocking collectives  340 us (32%)
  waiting for transfers between devices  279 us (26%)
  local copies, waits for them, and re-layouts  171 us (16%)
  matrix products  138 us (13%)
  other arithmetic  81.3 us (8%)
  starting transfers between devices  21.1 us (2%)
  between operations  15 us (1%)
    ppermute x4, waiting for transfers between devices, passed_along(): return lax.ppermute(block, axis, route)  154 us
    dot_general x16, matrix products, contract(): jnp.einsum(formula, table, data, precision=lax.Precision.HIGHEST, preferr...  138 us
    all_to_all x1, blocking collectives, per_device(): lax.all_to_all(misfit_pair, 'row', split_axis=2, concat_axis=1, tiled=True)  108 us
    all_to_all x1, blocking collectives, per_device(): lax.all_to_all(summed, 'row', split_axis=1, concat_axis=2, tiled=True)  106 us
    all_to_all x1, blocking collectives, per_device(): lax.all_to_all(adjoint, 'row', split_axis=2, concat_axis=3, tiled=True)  101 us
    all_to_all x1, waiting for transfers between devices, per_device(): lax.all_to_all(spectrum, 'row', split_axis=3, concat_axis=2, tiled=True)  85.5 us
    unnamed x2, waiting for transfers between devices  39.9 us
    reshape x2, local copies, waits for them, and re-layouts, transform_last(): result.reshape((result.shape[0],) + leading + (outer_len * inner_len,))  31.9 us
  transfers between devices with their start and end apart: 6, of which 5 were waited for; matrix products, arithmetic and copies ran while one was open for 3% of the time, Pallas kernels for 0%

profile of v1, /device:TPU:34, one launch (start us, length us, event | category | flops | bytes accessed | tf_op | source)
XLA Modules:
  0.0 1045.2 jit_solution(5366026882660989310)
XLA Ops:
  12.7 17.3 %fusion.101 = (f32[1,64,64,64]{2,3,0,1:T(8,128)S(1)}, f32[1,64,64,64]{2,3,0,1:T(8,128)}, f32[1,64,64,64]{2,3,0,1:T(8,128)}, f32[1,64,64,64]{2,3,0,1:T(8,128)}, f...) fusion(s32[64,64]{0,1:T(8,128)S(1)} %broadcast_multiply_fusion.3, s32[64,64]{1,0:T(8,128)S(1)} %copy.91), kind=kLoop, calls=%fused_computation.103 | loop fusion | flops 4980736 | bytes 6324224 | tf_op jit(solution)/shard_map/neg | solution.py:28
  38.1 11.0 %fusion.51 = f32[2,1,128,64,64]{2,3,0,4,1:T(8,128)S(1)} fusion(f32[1,2,64,64,64]{3,4,1,0,2:T(8,128)S(1)} %get-tuple-element.13, f32[1,2,64,64,64]{3,4,1,0,2:T(8,128)S(1)} %get-tuple-element.12, f32[2,128,64,64,1]{1,2,3,0,4:T(8,128)S(1)} %fusion.48), kind=kOutput, calls=%fused_computation.67 | convolution fusion | flops 1611661312 | bytes 12582912 | tf_op jit(solution)/shard_map/rqkbm,q...kb->r...mk/dot_general | solution.py:49
  51.6 16.2 %copy.95 = f32[2,1,128,4096]{2,0,1,3:T(2,128)} copy(f32[2,1,128,4096]{2,3,0,1:T(8,128)S(1)} %bitcast.249) | data formatting | bytes 8388608 | tf_op jit(solution)/shard_map/reshape | solution.py:65
  67.8 10.3 all-to-all-start
  79.2 8.6 fusion.43
  87.8 85.5 %all-to-all-done = f32[2,1,128,4096]{2,0,1,3:T(2,128)} async-done(((f32[2,1,128,4096]{2,0,1,3:T(2,128)}), f32[2,1,128,4096]{2,0,1,3:T(2,128)}, u32[]{:S(2)}, u32[]{:S(2)}) %all-to-all-start) | async-done | bytes 4194336 | tf_op jit(solution)/shard_map/all_to_all | solution.py:168
  183.5 8.8 fusion.54
  192.3 10.0 fusion.57
  202.3 8.3 multiply_add_fusion.1
  214.5 10.4 fusion.78
  227.3 15.6 %copy.105 = f32[2,4096,128]{2,0,1:T(2,128)S(1)} copy(f32[2,4096,128]{2,1,0:T(8,128)S(1)} %bitcast.252) | data formatting | bytes 8388608 | tf_op jit(solution)/shard_map/reshape | solution.py:78
  243.0 105.9 %all_to_all.65 = f32[2,4096,128]{2,0,1:T(2,128)S(1)} all-to-all(f32[2,4096,128]{2,0,1:T(2,128)S(1)} %copy.105), channel_id=1, replica_groups=mesh['depth'=8,'row'=32] {'row'}, dimensions={1} | all-to-all | bytes 8388608 | tf_op jit(solution)/shard_map/all_to_all | solution.py:173
  356.8 8.8 fusion.63
  378.3 39.8 %reduce-scatter.4.cloned.1.call-done = f32[16,4096]{1,0:T(8,128)} async-done(((f32[128,4096]{1,0:T(8,128)}), f32[16,4096]{1,0:T(8,128)}) %reduce-scatter.4.cloned.1.call-update) | async-done | bytes 262160
  426.5 24.9 %all_to_all.66 = f32[8,16,4096]{2,1,0:T(8,128)S(1)} all-to-all(f32[8,16,4096]{2,1,0:T(8,128)S(1)} %stack.118), channel_id=1, replica_groups=mesh['depth'=8,'row'=32] {'depth'}, dimensions={0} | all-to-all | bytes 4194304 | tf_op jit(solution)/shard_map/all_to_all | solution.py:178
  454.5 10.5 %fusion.44 = f32[2,128,64,64,1]{2,3,0,1,4:T(8,128)} fusion(f32[128,64,64]{2,1,0:T(8,128)} %reshape.609, f32[1,2,64,64]{3,2,1,0:T(8,128)S(1)} %get-tuple-element.24, f32[1,2,64,64]{3,2,1,0:T(8,128)S(1)} %get-tuple-element.25), kind=kOutput, calls=%fused_computation.62 | convolution fusion | flops 805314560 | bytes 6356992 | tf_op jit(solution)/shard_map/rqka,q...ab->r...kb/dot_general | solution.py:49
  465.0 8.8 copy.155
  473.8 10.6 %fusion.47 = f32[2,128,64,64]{1,2,0,3:T(8,128)S(1)} fusion(f32[2,128,64,64,1]{1,3,0,4,2:T(8,128)} %copy.155, f32[1,2,64,64,64]{3,4,1,0,2:T(8,128)} %copy-done.5, f32[1,2,64,64,64]{3,4,1,0,2:T(8,128)} %copy-done.2), kind=kOutput, calls=%fused_computation.65 | convolution fusion | flops 1611661312 | bytes 12582912 | tf_op jit(solution)/shard_map/rqkbm,q...kb->r...mk/dot_general | solution.py:49
  486.9 15.6 %copy.116 = f32[2,128,4096]{1,0,2:T(2,128)S(1)} copy(f32[2,128,4096]{1,2,0:T(8,128)S(1)} %bitcast.255) | data formatting | bytes 8388608 | tf_op jit(solution)/shard_map/reshape | solution.py:65
  502.5 107.6 %all_to_all.67 = f32[2,128,4096]{1,0,2:T(2,128)S(1)} all-to-all(f32[2,128,4096]{1,0,2:T(2,128)S(1)} %copy.116), channel_id=1, replica_groups=mesh['depth'=8,'row'=32] {'row'}, dimensions={2} | all-to-all | bytes 8388608 | tf_op jit(solution)/shard_map/all_to_all | solution.py:181
  618.1 8.7 fusion.66
  626.8 10.0 fusion.69
  636.8 8.3 multiply_subtract_fusion
  649.2 10.4 fusion.83
  662.0 15.6 %copy.126 = f32[2,1,4096,128]{3,0,1,2:T(2,128)S(1)} copy(f32[2,1,4096,128]{3,2,0,1:T(8,128)S(1)} %bitcast.257) | data formatting | bytes 8388608 | tf_op jit(solution)/shard_map/reshape | solution.py:78
  677.6 101.2 %all_to_all.68 = f32[2,1,4096,128]{3,0,1,2:T(2,128)S(1)} all-to-all(f32[2,1,4096,128]{3,0,1,2:T(2,128)S(1)} %copy.126), channel_id=1, replica_groups=mesh['depth'=8,'row'=32] {'row'}, dimensions={2} | all-to-all | bytes 8388608 | tf_op jit(solution)/shard_map/all_to_all | solution.py:186
  786.7 8.8 fusion.75
  795.6 10.0 fusion.13
  832.8 71.7 %collective-permute-done = f32[2,1,128,4096]{2,3,0,1:T(8,128)} collective-permute-done((f32[2,1,128,4096]{2,3,0,1:T(8,128)}, f32[2,1,128,4096]{2,3,0,1:T(8,128)}, u32[]{:S(2)}, u32[]{:S(2)}) %collective-permute-start) | collective-permute-done | bytes 4194336 | tf_op jit(solution)/shard_map/ppermute | solution.py:14
  904.4 9.1 add_reduce_fusion
  939.5 78.9 %collective-permute-done.2 = f32[2,1,128,4096]{2,3,0,1:T(8,128)} collective-permute-done((f32[2,1,128,4096]{2,3,0,1:T(8,128)}, f32[2,1,128,4096]{2,3,0,1:T(8,128)}, u32[]{:S(2)}, u32[]{:S(2)}) %collective-permute-start.2) | collective-permute-done | bytes 4194336 | tf_op jit(solution)/shard_map/ppermute | solution.py:14
  1018.4 13.9 %fusion.10 = f32[2,1,128,4096]{2,3,0,1:T(8,128)} fusion(f32[2,1,128,4096]{2,3,0,1:T(8,128)} %bitcast_subtract_fusion, f32[2,1,128,4096]{2,3,0,1:T(8,128)} %copy-done.8, f32[2,1,127,4096]{2,3,0,1:T(8,128)} %bitcast.244, f32[2,1,1,4096]{2,3,0,1:T(8,128)} %copy.137, f32[2,1,128,4096]{2,3,0,1:T(8,128)} %get-tuple-element.7, f32[2,1,128,4095]{2,3,0,1:T(8,128)} %bitcast.245, ...), kind=kLoop, calls=%fused_computation.21 | loop fusion | flops 8388608 | bytes 33553408 | tf_op jit(solution)/shard_map/add | solution.py:146
  (104 shorter events, 148.9 us)
Async XLA Ops:
  6.5 371.1 %copy-start = (f32[128,4096]{1,0:T(8,128)S(1)}, f32[128,4096]{1,0:T(8,128)}, u32[]{:S(2)}) copy-start(f32[128,4096]{1,0:T(8,128)} %param.4) | copy-start | bytes 6291460
  30.0 2.2 copy-start.15
  31.7 6.4 copy-start.2
  31.7 6.4 copy-start.5
  67.8 105.6 %all-to-all-start = ((f32[2,1,128,4096]{2,0,1,3:T(2,128)}), f32[2,1,128,4096]{2,0,1,3:T(2,128)}, u32[]{:S(2)}, u32[]{:S(2)}) async-start(f32[2,1,128,4096]{2,0,1,3:T(2,128)} %copy.95), calls=%async_computation | async-start | bytes 8388608 | tf_op jit(solution)/shard_map/all_to_all | solution.py:168
  78.1 340.0 %reduce-scatter.4.cloned.1.call-start = ((), (), s32[]{:S(2)}) async-start(), calls=%async_computation.6 | async-start | bytes 2359296
  183.5 8.8 copy-start.3
  183.5 8.8 copy-start.6
  210.6 3.9 copy-start.9
  210.6 3.9 copy-start.12
  356.8 8.8 copy-start.20
  356.8 8.8 copy-start.21
  618.1 8.7 copy-start.4
  618.1 8.7 copy-start.7
  645.1 4.1 copy-start.10
  645.1 4.1 copy-start.13
  786.7 8.8 copy-start.11
  786.7 8.8 copy-start.14
  805.6 2.7 copy-start.16
  810.6 93.8 %collective-permute-start = (f32[2,1,128,4096]{2,3,0,1:T(8,128)}, f32[2,1,128,4096]{2,3,0,1:T(8,128)}, u32[]{:S(2)}, u32[]{:S(2)}) collective-permute-start(f32[2,1,128,4096]{2,3,0,1:T(8,128)} %bitcast_subtract_fusion), channel_id=1, source_target_pairs={{32,0},{64,32},{96,64},{128,96},{160,128},{192,160},{224,192},{33,... | collective-permute-start | bytes 12582920 | tf_op jit(solution)/shard_map/ppermute | solution.py:14
  817.6 12.5 %collective-permute-start.1 = (f32[2,1,1,4096]{3,0,2,1:T(2,128)S(1)}, f32[2,1,1,4096]{3,0,2,1:T(2,128)S(1)}, u32[]{:S(2)}, u32[]{:S(2)}) collective-permute-start(f32[2,1,1,4096]{3,0,2,1:T(2,128)S(1)} %copy.134), channel_id=1, source_target_pairs={{1,0},{2,1},{3,2},{4,3},{5,4},{6,5},{7,6},{8,7},{9,8},{10,9},{11,1... | collective-permute-start | bytes 98312 | tf_op jit(solution)/shard_map/ppermute | solution.py:14
  904.4 9.9 copy-start.18
  904.4 9.9 copy-start.19
  913.5 2.3 copy-start.17
  923.0 2.7 copy-start.8
  923.0 95.5 %collective-permute-start.2 = (f32[2,1,128,4096]{2,3,0,1:T(8,128)}, f32[2,1,128,4096]{2,3,0,1:T(8,128)}, u32[]{:S(2)}, u32[]{:S(2)}) collective-permute-start(f32[2,1,128,4096]{2,3,0,1:T(8,128)} %get-tuple-element.5), channel_id=1, source_target_pairs={{0,32},{32,64},{64,96},{96,128},{128,160},{160,192},{192,224},{1,3... | collective-permute-start | bytes 12582920 | tf_op jit(solution)/shard_map/ppermute | solution.py:14
  931.7 5.2 collective-permute-start.3
  1018.4 19.5 %copy-start.1 = (f32[128,4096]{1,0:T(8,128)S(1)}, f32[128,4096]{1,0:T(8,128)}, u32[]{:S(2)}) copy-start(f32[128,4096]{1,0:T(8,128)} %param.4) | copy-start | bytes 6291460
Sparse Core Ops, SparseCore 0:
  377.7 40.3 reduce-scatter.3
